TPU v7x, 32 devices: a whole 2x2x4 slice. The times are simulated.
32 devices in a mesh: grid: 4 (over z), band: 4 (over y, x), atom: 2 (over core).
Axes of the slice: x: 2, y: 2, z: 4, core: 2. Of those that a mesh axis runs over, the one named last changes fastest.
Arguments:
- psi: float32 [256, 64, 1024], P('band', 'grid'), may hold values from -27 to 27
- potential: float32 [64, 1024], P(('grid', 'atom')), may hold values from -12 to 12
- projectors: float32 [128, 4, 512], P('grid'), may hold values from -5 to 5
- strength: float32 [128, 4], P('grid'), may hold values from 0.5 to 8
- sphere_index: int32 [128, 512], P('grid'), may hold values from 2048 to 25599, as said below
- atom_count: int32 [4], P('grid'), may hold values from 2 to 32, as said below
Outputs:
- orthonormal: float32 [256, 64, 1024], P('band', ('grid', 'atom'))
Inputs may be any that keep to these rules, and one draw needn't show every extreme that they name: `sphere_index`: row a lists the 512 cells of an 8 x 8 x 8 cube about the atom's centre, offsets -4 to 3 in each direction, as e * 1024 + x * 32 + y with e counted from 6 rows below its domain. `atom_count`: the live slots of a domain are its first ones; in every draw some domain has all 32 live.
All inputs are finite; a program needn't handle non-finite values.
Results may differ from a plain program's by a relative error of at most 0.0003.
Values sent between devices are 32-bit elements; how exact they have to be, the bound alone decides.
A program may use at most 128 MiB of HBM per device.

v0:
```python
import math
import jax
import jax.numpy as jnp
from jax import lax
from jax.sharding import PartitionSpec as P

BANDS = 256
CY = 32
STENCIL = (
    -5369.0 / 1800.0,
    12.0 / 7.0,
    -15.0 / 56.0,
    10.0 / 189.0,
    -1.0 / 112.0,
    2.0 / 1925.0,
    -1.0 / 16632.0,
)
KINETIC = -0.5 * 4.0
STEP_SIZE = 0.05
HIGHEST = lax.Precision.HIGHEST


def from_behind(block, axis, distance):
    devices = range(lax.axis_size(axis))
    route = [((i - distance) % len(devices), i) for i in devices]
    return lax.ppermute(block, axis, route)


def extended_2(x, sides, width):
    for axis, dim in sides:
        count, length = (lax.axis_size(axis), x.shape[dim])
        up = [(i, (i + 1) % count) for i in range(count)]
        down = [(j, i) for i, j in up]
        last = lax.slice_in_dim(x, length - width, length, axis=dim)
        first = lax.slice_in_dim(x, 0, width, axis=dim)
        before = lax.ppermute(last, axis, up)
        after = lax.ppermute(first, axis, down)
        x = jnp.concatenate([before, x, after], axis=dim)
    return x


def inner_rows(left, right):
    return lax.dot_general(
        left, right, (((1,), (1,)), ((), ())), precision=HIGHEST, preferred_element_type=jnp.float32
    )


def spread_terms(weighted, projectors, sphere_index, total_cells):
    band_rows = weighted.shape[0]
    values = jnp.einsum("nai,ais->nas", weighted, projectors, precision=HIGHEST)
    dense = jnp.zeros((band_rows, total_cells), jnp.float32)
    return dense.at[:, sphere_index.reshape(-1)].add(values.reshape(band_rows, -1))


def fold_rims(dense, depth):
    from_below = from_behind(dense[:, depth + 6 :], "grid", 1)
    from_above = from_behind(dense[:, :6], "grid", -1)
    inner = dense[:, 6 : depth + 6]
    inner = inner.at[:, :6].add(from_below)
    return inner.at[:, depth - 6 :].add(from_above)


def body(psi, potential, projectors, strength, sphere_index, atom_count):
    band_rows, depth, plane_cells = psi.shape
    groups = lax.axis_size("atom")
    core = lax.axis_index("atom")
    half = depth // groups
    extended = extended_2(psi, (("grid", 1),), 6)
    window = lax.dynamic_slice_in_dim(extended, core * half, half + 12, 1)
    centre = window[:, 6 : 6 + half]
    margin = 6 * CY
    padded = jnp.pad(centre, ((0, 0), (0, 0), (margin, margin)))
    column = lax.iota(jnp.int32, plane_cells) % CY
    laplace = 3.0 * STENCIL[0] * centre
    for k in range(1, 7):
        along_z = window[:, 6 + k : 6 + k + half] + window[:, 6 - k : 6 - k + half]
        along_x = (
            padded[:, :, margin + k * CY : margin + k * CY + plane_cells]
            + padded[:, :, margin - k * CY : margin - k * CY + plane_cells]
        )
        upper = jnp.where(column + k < CY, padded[:, :, margin + k : margin + k + plane_cells], 0.0)
        lower = jnp.where(column >= k, padded[:, :, margin - k : margin - k + plane_cells], 0.0)
        laplace = laplace + STENCIL[k] * (along_z + along_x + upper + lower)
    atom_slots = sphere_index.shape[0]
    share = atom_slots // groups
    alive_mask = (lax.iota(jnp.int32, atom_slots) < atom_count[0]).astype(jnp.float32)
    scaled = strength * alive_mask[:, None]
    flattened = extended.reshape(band_rows, -1)
    total_cells = flattened.shape[1]
    own_index = lax.dynamic_slice_in_dim(sphere_index, core * share, share, 0)
    own_projectors = lax.dynamic_slice_in_dim(projectors, core * share, share, 0)
    own_scaled = lax.dynamic_slice_in_dim(scaled, core * share, share, 0)
    points = flattened[:, own_index]
    intersections = jnp.einsum(
        "nas,ais->nai", points, own_projectors, precision=HIGHEST
    ) / math.sqrt(projectors.shape[2])
    weighted = intersections * own_scaled[None]
    dense = spread_terms(weighted, own_projectors, own_index, total_cells).reshape(
        band_rows, depth + 12, plane_cells
    )
    nonlocal_half = lax.psum_scatter(
        fold_rims(dense, depth), "atom", scatter_dimension=1, tiled=True
    )
    updated = centre - STEP_SIZE * (KINETIC * laplace + potential * centre + nonlocal_half)
    flat_rows = updated.reshape(band_rows, half * plane_cells)
    cells_total = lax.axis_size("grid") * depth * plane_cells
    block = inner_rows(flat_rows, lax.all_gather(flat_rows, "band", axis=0, tiled=True))
    summed_rows = lax.psum(block, ("grid", "atom")) / cells_total
    intersection_matrix = lax.all_gather(summed_rows, "band", axis=0, tiled=True)
    factor = jnp.linalg.cholesky(intersection_matrix)
    inverse = lax.linalg.triangular_solve(
        factor, jnp.eye(BANDS, dtype=jnp.float32), left_side=True, lower=True
    )
    own_inverse = lax.dynamic_slice_in_dim(
        inverse, lax.axis_index("band") * band_rows, band_rows, 0
    )
    result = jnp.dot(
        own_inverse,
        lax.all_gather(flat_rows, "band", axis=0, tiled=True),
        precision=HIGHEST,
        preferred_element_type=jnp.float32,
    )
    return result.reshape(band_rows, half, plane_cells)


def solution(mesh):
    in_specs = (
        P("band", "grid", None),
        P(("grid", "atom"), None),
        P("grid", None, None),
        P("grid", None),
        P("grid", None),
        P("grid"),
    )
    out_specs = P("band", ("grid", "atom"), None)
    return jax.shard_map(body, mesh=mesh, in_specs=in_specs, out_specs=out_specs, check_vma=False)
```

profile of v0, /device:TPU:0, one launch (start us, length us, event | category | flops | bytes accessed | tf_op | source)
XLA Modules:
  0.0 547.4 jit_solution(13201074883905596832)
XLA Ops:
  6.5 2.7 fusion.95
  9.3 0.9 copy.62
  10.2 3.1 collective-permute-start
  13.3 0.9 copy.63
  14.2 2.4 collective-permute-start.1
  17.4 0.1 fusion.91
  17.5 0.1 copy.43
  17.6 33.1 %collective-permute-done = f32[64,6,1024]{2,0,1:T(8,128)} collective-permute-done((f32[64,6,1024]{2,0,1:T(8,128)S(1)}, f32[64,6,1024]{2,0,1:T(8,128)}, u32[]{:S(2)}, u32[]{:S(2)}) %collective-permute-start) | collective-permute-done | bytes 1572896 | tf_op jit(solution)/shard_map/ppermute | solution.py:36
  50.7 2.7 constant_dynamic-update-slice_fusion.2
  53.5 6.6 %constant_dynamic-update-slice_fusion.1 = f32[64,28,1024]{2,0,1:T(8,128)} fusion(f32[64,28,1024]{2,0,1:T(8,128)} %constant_dynamic-update-slice_fusion.2, f32[64,16,1024]{2,1,0:T(8,128)} %param.10), kind=kLoop, calls=%fused_computation.132 | loop fusion | bytes 8388608
  60.1 23.5 %collective-permute-done.1 = f32[64,6,1024]{2,0,1:T(8,128)} collective-permute-done((f32[64,6,1024]{2,0,1:T(8,128)S(1)}, f32[64,6,1024]{2,0,1:T(8,128)}, u32[]{:S(2)}, u32[]{:S(2)}) %collective-permute-start.1) | collective-permute-done | bytes 1572896 | tf_op jit(solution)/shard_map/ppermute | solution.py:37
  83.5 2.8 constant_dynamic-update-slice_fusion
  86.4 11.1 %copy.41 = f32[64,28,1024]{0,2,1:T(8,128)} copy(f32[64,28,1024]{2,0,1:T(8,128)} %constant_dynamic-update-slice_fusion) | data formatting | bytes 14680064 | tf_op jit(solution)/shard_map/concatenate | solution.py:38
  97.5 32.9 %gather_fusion = f32[8192,64]{1,0:T(8,128)} fusion(f32[64,28672]{0,1:T(8,128)} %bitcast.71, s32[8192]{0:T(1024)S(1)} %broadcast_clamp_fusion), kind=kCustom, calls=%fused_computation | custom fusion | bytes 4227072 | tf_op jit(solution)/shard_map/gather | solution.py:93
  130.4 2.8 copy.42
  133.2 1.8 fusion.62
  135.1 1.9 convolution_bitcast_fusion
  136.9 0.2 copy.56
  137.2 2.7 copy.45
  139.9 50.9 %scatter_custom_fusion = f32[64,28672]{0,1:T(8,128)} fusion(s32[8192]{0:T(1024)S(1)} %bitcast.79, f32[8192,64]{1,0:T(8,128)} %copy.45, f32[]{:T(128)} %constant.181.clone.1), kind=kCustom, calls=%fused_computation.28 | custom fusion | flops 524288 | bytes 7340544 | tf_op jit(solution)/shard_map/scatter-add | solution.py:52
  190.8 7.1 %fusion.94 = (f32[64,6,1024]{0,2,1:T(8,128)}, f32[64,6,1024]{0,2,1:T(8,128)}, f32[64,6,1024]{0,2,1:T(8,128)S(1)}) fusion(f32[64,28,1024]{0,2,1:T(8,128)} %bitcast.69), kind=kLoop, calls=%fused_computation.166 | loop fusion | bytes 9437184 | tf_op jit(solution)/shard_map/slice | solution.py:57
  197.8 3.2 copy.54
  201.1 0.6 collective-permute-start.2
  201.6 3.2 copy.55
  204.9 10.5 %collective-permute-start.3 = (f32[64,6,1024]{2,0,1:T(8,128)}, f32[64,6,1024]{2,0,1:T(8,128)}, u32[]{:S(2)}, u32[]{:S(2)}) collective-permute-start(f32[64,6,1024]{2,0,1:T(8,128)} %copy.55), channel_id=1, source_target_pairs={{8,0},{16,8},{24,16},{0,24},{9,1},{17,9},{25,17},{1,25},{10,2},{18... | collective-permute-start | bytes 4718600 | tf_op jit(solution)/shard_map/ppermute | solution.py:26
  215.4 7.5 %slice.277 = f32[64,16,1024]{0,2,1:T(8,128)} slice(f32[64,28,1024]{0,2,1:T(8,128)} %bitcast.70), slice={[0:64], [6:22], [0:1024]} | slice | bytes 8388608 | tf_op jit(solution)/shard_map/slice | solution.py:58
  222.8 2.0 copy.53
  224.9 6.9 %copy.52 = f32[64,16,1024]{2,0,1:T(8,128)} copy(f32[64,16,1024]{0,2,1:T(8,128)} %slice.277) | data formatting | bytes 8388608
  231.8 16.0 %collective-permute-done.2 = f32[64,6,1024]{2,0,1:T(8,128)} collective-permute-done((f32[64,6,1024]{2,0,1:T(8,128)}, f32[64,6,1024]{2,0,1:T(8,128)}, u32[]{:S(2)}, u32[]{:S(2)}) %collective-permute-start.2) | collective-permute-done | bytes 1572896 | tf_op jit(solution)/shard_map/ppermute | solution.py:26
  247.7 2.8 add_dynamic-update-slice_fusion
  250.6 22.7 %collective-permute-done.3 = f32[64,6,1024]{2,0,1:T(8,128)} collective-permute-done((f32[64,6,1024]{2,0,1:T(8,128)}, f32[64,6,1024]{2,0,1:T(8,128)}, u32[]{:S(2)}, u32[]{:S(2)}) %collective-permute-start.3) | collective-permute-done | bytes 1572896 | tf_op jit(solution)/shard_map/ppermute | solution.py:26
  273.2 3.4 fusion.58
  276.6 0.0 reduce-scatter.2.cloned.1.call-update
  276.7 0.0 all-gather.2.cloned.1.call-start
  276.8 1.7 constant_dynamic-slice_fusion.1
  278.5 8.5 %reduce-scatter.2.cloned.1.call-done = f32[64,8,1024]{2,0,1:T(8,128)} async-done(((f32[64,16,1024]{2,0,1:T(8,128)}), f32[64,8,1024]{2,0,1:T(8,128)}) %reduce-scatter.2.cloned.1.call-update) | async-done | bytes 2097168 | tf_op jit(solution)/shard_map/reduce_scatter | solution.py:101
  287.1 15.7 %fusion.57 = f32[8,8,8,1024]{3,2,1,0:T(8,128)S(1)} fusion(f32[64,8,1024]{2,0,1:T(8,128)S(1)} %constant_dynamic-slice_fusion.1, f32[64,8,1024]{2,0,1:T(8,128)} %reduce-scatter.2.cloned.1.call-done, f32[64,28,1024]{2,0,1:T(8,128)} %constant_dynamic-update-slice_fusion, s32[]{:T(128)S(6)} %select_n.94, s32[]{:T(128)S(6)} %add.301, s32[]{:T(128)S(6)} %add.300, ...), kind=kLoop, calls=%fused_computation.91 | loop fusion | flops 31981568 | bytes 31502384
  302.8 1.6 copy.57
  304.4 0.0 all-reduce.4.cloned.1.call-start
  304.5 88.8 %all-gather.2.cloned.1.call-done = f32[256,8192]{1,0:T(8,128)} async-done(((f32[64,8192]{1,0:T(8,128)}), f32[256,8192]{1,0:T(8,128)}) %all-gather.2.cloned.1.call-update) | async-done | bytes 8388624 | tf_op jit(solution)/shard_map/all_gather | solution.py:107
  393.3 10.7 %fusion.96 = f32[64,256]{1,0:T(8,128)} fusion(f32[64,8192]{1,0:T(8,128)S(1)} %bitcast.73, f32[256,8192]{1,0:T(8,128)} %all-gather.2.cloned.1.call-done), kind=kOutput, calls=%fused_computation.168 | convolution fusion | flops 1610612736 | bytes 10551296 | tf_op jit(solution)/shard_map/dot_general | solution.py:43
  404.1 54.8 %all-reduce.4.cloned.1.call-done = f32[64,256]{1,0:T(8,128)} async-done(((f32[64,256]{1,0:T(8,128)}), f32[64,256]{1,0:T(8,128)}) %all-reduce.4.cloned.1.call-update) | async-done | bytes 65552 | tf_op jit(solution)/shard_map/psum | solution.py:108
  458.9 0.8 broadcast_multiply_fusion
  459.7 9.4 %all_gather.8 = f32[256,256]{1,0:T(8,128)S(1)} all-gather(f32[64,256]{1,0:T(8,128)S(1)} %broadcast_multiply_fusion), channel_id=1, replica_groups=mesh['grid'=4,'band'=4,'atom'=2] {'band'}, dimensions={0}, use_global_device_ids=true | all-gather | bytes 327680 | tf_op jit(solution)/shard_map/all_gather | solution.py:109
  469.2 0.1 copy.51
  469.4 11.7 %cholesky.50 = f32[128,128]{1,0:T(8,128)S(1)} custom-call(f32[128,128]{1,0:T(8,128)S(1)} %cholesky.118), custom_call_target="Cholesky" | custom-call | tf_op jit(solution)/shard_map/jit(cholesky)/cholesky | solution.py:110
  481.2 9.8 %custom-call.14 = f32[1,128,128]{1,2,0:T(8,128)S(1)} custom-call(f32[1,128,128]{2,1,0:T(8,128)S(1)} %get-tuple-element.55), custom_call_target="InvertDiagBlocksLowerTriangular" | custom-call | tf_op jit(solution)/shard_map/jit(cholesky)/cholesky | solution.py:110
  491.0 0.2 constant_dynamic-update-slice_fusion.3
  491.2 0.3 convolution_subtract_fusion.1
  491.4 11.7 %cholesky.105 = f32[128,128]{1,0:T(8,128)S(1)} custom-call(f32[128,128]{1,0:T(8,128)S(1)} %convolution_subtract_fusion.1), custom_call_target="Cholesky" | custom-call | tf_op jit(solution)/shard_map/jit(cholesky)/cholesky | solution.py:110
  503.2 0.7 compare_reduce_fusion
  503.9 0.6 compare_reduce_fusion.1
  505.8 0.1 triangular_solve.63
  505.9 4.1 while.3
  506.1 0.6 fusion.106
  506.7 1.4 bitcast_dynamic-update-slice_fusion.2
  508.1 0.6 fusion.106
  508.7 1.4 bitcast_dynamic-update-slice_fusion.2
  510.1 19.7 %custom-call.15 = f32[2,128,128]{1,2,0:T(8,128)S(1)} custom-call(f32[2,128,128]{2,1,0:T(8,128)S(1)} %get-tuple-element.36), custom_call_target="InvertDiagBlocksLowerTriangular" | custom-call | tf_op jit(solution)/shard_map/triangular_solve | solution.py:111
  529.7 0.3 fusion.66
  530.0 0.3 convolution_subtract_fusion
  530.3 0.3 fusion.74
  530.6 7.5 %fusion.71 = f32[64,8192]{1,0:T(8,128)S(1)} fusion(f32[256,8192]{1,0:T(8,128)} %all-gather.2.cloned.1.call-done, s32[]{:T(128)S(6)} %select_n.112, f32[128,256]{1,0:T(8,128)S(1)} %fusion.66, f32[128,256]{1,0:T(8,128)S(1)} %fusion.74), kind=kOutput, calls=%fused_computation.114 | convolution fusion | flops 1610629120 | bytes 10747908 | tf_op jit(solution)/shard_map/dot_general | solution.py:117
  538.1 2.5 copy.60
  (41 shorter events, 0.4 us)
Async XLA Ops:
  6.5 126.7 %copy-start = (f32[32,4,512]{2,1,0:T(4,128)S(1)}, f32[32,4,512]{2,1,0:T(4,128)}, u32[]{:S(2)}) copy-start(f32[32,4,512]{2,1,0:T(4,128)} %param.12) | copy-start | bytes 786436
  6.5 280.5 %reduce-scatter.2.cloned.1.call-start = ((), (), s32[]{:S(2)}) async-start(), calls=%async_computation.1 | async-start | bytes 6291456 | tf_op jit(solution)/shard_map/reduce_scatter | solution.py:101
  10.2 6.4 %copy-start.5 = (s32[32,512]{1,0:T(8,128)S(1)}, s32[32,512]{1,0:T(8,128)}, u32[]{:S(2)}) copy-start(s32[32,512]{1,0:T(8,128)} %param.14) | copy-start | bytes 196612
  10.2 7.2 %copy-start.6 = (f32[32,4]{0,1:T(4,128)S(1)}, f32[32,4]{0,1:T(4,128)}, u32[]{:S(2)}) copy-start(f32[32,4]{0,1:T(4,128)} %param.13) | copy-start | bytes 1540
  10.2 40.5 %collective-permute-start = (f32[64,6,1024]{2,0,1:T(8,128)S(1)}, f32[64,6,1024]{2,0,1:T(8,128)}, u32[]{:S(2)}, u32[]{:S(2)}) collective-permute-start(f32[64,6,1024]{2,0,1:T(8,128)S(1)} %copy.62), channel_id=1, source_target_pairs={{0,8},{8,16},{16,24},{24,0},{1,9},{9,17},{17,25},{25,1},{2,10},{10... | collective-permute-start | bytes 4718600 | tf_op jit(solution)/shard_map/ppermute | solution.py:36
  14.2 69.3 %collective-permute-start.1 = (f32[64,6,1024]{2,0,1:T(8,128)S(1)}, f32[64,6,1024]{2,0,1:T(8,128)}, u32[]{:S(2)}, u32[]{:S(2)}) collective-permute-start(f32[64,6,1024]{2,0,1:T(8,128)S(1)} %copy.63), channel_id=1, source_target_pairs={{8,0},{16,8},{24,16},{0,24},{9,1},{17,9},{25,17},{1,25},{10,2},{18... | collective-permute-start | bytes 4718600 | tf_op jit(solution)/shard_map/ppermute | solution.py:37
  201.1 46.6 %collective-permute-start.2 = (f32[64,6,1024]{2,0,1:T(8,128)}, f32[64,6,1024]{2,0,1:T(8,128)}, u32[]{:S(2)}, u32[]{:S(2)}) collective-permute-start(f32[64,6,1024]{2,0,1:T(8,128)} %copy.54), channel_id=1, source_target_pairs={{24,0},{0,8},{8,16},{16,24},{25,1},{1,9},{9,17},{17,25},{26,2},{2,... | collective-permute-start | bytes 4718600 | tf_op jit(solution)/shard_map/ppermute | solution.py:26
  204.9 68.4 %collective-permute-start.3 = (f32[64,6,1024]{2,0,1:T(8,128)}, f32[64,6,1024]{2,0,1:T(8,128)}, u32[]{:S(2)}, u32[]{:S(2)}) collective-permute-start(f32[64,6,1024]{2,0,1:T(8,128)} %copy.55), channel_id=1, source_target_pairs={{8,0},{16,8},{24,16},{0,24},{9,1},{17,9},{25,17},{1,25},{10,2},{18... | collective-permute-start | bytes 4718600 | tf_op jit(solution)/shard_map/ppermute | solution.py:26
  224.9 22.9 %copy-start.3 = (f32[64,6,1024]{2,0,1:T(8,128)S(1)}, f32[64,6,1024]{2,0,1:T(8,128)}, u32[]{:S(2)}) copy-start(f32[64,6,1024]{2,0,1:T(8,128)} %copy.53) | copy-start | bytes 4718596
  276.7 116.6 %all-gather.2.cloned.1.call-start = ((), (), s32[]{:S(2)}) async-start(), calls=%async_computation.2 | async-start | bytes 10485760 | tf_op jit(solution)/shard_map/all_gather | solution.py:107
  276.8 10.3 %copy-start.4 = (f32[8,1024]{1,0:T(8,128)S(1)}, f32[8,1024]{1,0:T(8,128)}, u32[]{:S(2)}) copy-start(f32[8,1024]{1,0:T(8,128)} %param.11) | copy-start | bytes 98308
  304.3 89.0 %copy-start.2 = (f32[8,8,8,1024]{3,2,0,1:T(8,128)S(1)}, f32[8,8,8,1024]{3,2,0,1:T(8,128)}, u32[]{:S(2)}) copy-start(f32[8,8,8,1024]{3,2,0,1:T(8,128)} %copy.57) | copy-start | bytes 6291460
  304.4 154.5 %all-reduce.4.cloned.1.call-start = ((), (), s32[]{:S(2)}) async-start(), calls=%async_computation.3 | async-start | bytes 131072 | tf_op jit(solution)/shard_map/psum | solution.py:108
  538.1 2.5 copy-start.1
Sparse Core Ops, SparseCore 0:
  276.8 10.2 reduce-scatter.1
  304.5 88.7 all-gather.1
  404.2 54.6 all-reduce.3
where the time goes:
time: 551 us; the launch traced here: 547 us
  waiting for transfers between devices  247 us (45%)
  other arithmetic  128 us (23%)
  local copies, waits for them, and re-layouts  107 us (19%)
  matrix products  23.2 us (4%)
  starting transfers between devices  16.7 us (3%)
  between operations  15.6 us (3%)
  blocking collectives  9.45 us (2%)
    all_gather x1, waiting for transfers between devices, body(): lax.all_gather(flat_rows, 'band', axis=0, tiled=True)  88.8 us
    psum x1, waiting for transfers between devices, body(): summed_rows = lax.psum(block, ('grid', 'atom')) / cells_total  54.8 us
    scatter-add x1, other arithmetic, spread_terms(): dense.at[:, sphere_index.reshape(-1)].add(values.reshape(band_rows, -1))  50.9 us
    ppermute x2, waiting for transfers between devices, from_behind(): return lax.ppermute(block, axis, route)  38.6 us
    gather x2, local copies, waits for them, and re-layouts, body(): points = flattened[:, own_index]  35.8 us
    another operation x7, other arithmetic, body(): factor = jnp.linalg.cholesky(intersection_matrix)  34.6 us
    ppermute x1, waiting for transfers between devices, extended_2(): before = lax.ppermute(last, axis, up)  33.1 us
    unnamed x25, local copies, waits for them, and re-layouts  29.1 us
  transfers between devices with their start and end apart: 7, of which 7 were waited for; matrix products, arithmetic and copies ran while one was open for 6% of the time, Pallas kernels for 0%

commit v1 on v0

--- a/solution.py
+++ b/solution.py
@@ -18,6 +18,11 @@
 KINETIC = -0.5 * 4.0
 STEP_SIZE = 0.05
 HIGHEST = lax.Precision.HIGHEST
+
+
+def add_all(x, name):
+    parts = lax.all_gather(x, name)
+    return jnp.sum(parts, axis=0)
 
 
 def from_behind(block, axis, distance):
@@ -105,7 +110,7 @@
     flat_rows = updated.reshape(band_rows, half * plane_cells)
     cells_total = lax.axis_size("grid") * depth * plane_cells
     block = inner_rows(flat_rows, lax.all_gather(flat_rows, "band", axis=0, tiled=True))
-    summed_rows = lax.psum(block, ("grid", "atom")) / cells_total
+    summed_rows = add_all(block, ("grid", "atom")) / cells_total
     intersection_matrix = lax.all_gather(summed_rows, "band", axis=0, tiled=True)
     factor = jnp.linalg.cholesky(intersection_matrix)
     inverse = lax.linalg.triangular_solve(

time: 551 us -> 509 us (0.924)
  waiting for transfers between devices: 247 us -> 193 us
  blocking collectives: 9.45 us -> 23.9 us
    psum x1 -> x0, waiting for transfers between devices: 54.8 us -> none  [body(): summed_rows = lax.psum(block, ('grid', 'atom')) / cells_total]
    all_gather x0 -> x1, blocking collectives: none -> 14.7 us  [add_all(): parts = lax.all_gather(x, name)]
  transfers between devices with their start and end apart: 7 -> 6, of which waited for: 7 -> 6; matrix products, arithmetic and copies ran while one was open for 6% -> 7% of each run, Pallas kernels for 0% -> 0%
where the time goes in v1:
time: 509 us; the launch traced here: 506 us
  waiting for transfers between devices  193 us (38%)
  other arithmetic  127 us (25%)
  local copies, waits for them, and re-layouts  107 us (21%)
  blocking collectives  23.9 us (5%)
  matrix products  22.6 us (4%)
  starting transfers between devices  16.6 us (3%)
  between operations  15.9 us (3%)
    all_gather x1, waiting for transfers between devices, body(): lax.all_gather(flat_rows, 'band', axis=0, tiled=True)  88.9 us
    scatter-add x1, other arithmetic, spread_terms(): dense.at[:, sphere_index.reshape(-1)].add(values.reshape(band_rows, -1))  50.9 us
    ppermute x2, waiting for transfers between devices, from_behind(): return lax.ppermute(block, axis, route)  38.6 us
    gather x2, local copies, waits for them, and re-layouts, body(): points = flattened[:, own_index]  35.9 us
    another operation x7, other arithmetic, body(): factor = jnp.linalg.cholesky(intersection_matrix)  34.6 us
    ppermute x1, waiting for transfers between devices, extended_2(): before = lax.ppermute(last, axis, up)  33.1 us
    unnamed x25, local copies, waits for them, and re-layouts  29.2 us
    ppermute x1, waiting for transfers between devices, extended_2(): after = lax.ppermute(first, axis, down)  23.4 us
  transfers between devices with their start and end apart: 6, of which 6 were waited for; matrix products, arithmetic and copies ran while one was open for 7% of the time, Pallas kernels for 0%

profile of v1, /device:TPU:0, one launch (start us, length us, event | category | flops | bytes accessed | tf_op | source)
XLA Modules:
  0.0 506.0 jit_solution(9715899000092682319)
XLA Ops:
  6.5 2.7 fusion.95
  9.3 0.9 copy.60
  10.2 0.0 copy-start.6
  10.2 3.1 collective-permute-start
  13.3 0.9 copy.61
  14.2 2.4 collective-permute-start.1
  17.4 0.1 fusion.91
  17.5 0.1 copy.41
  17.6 33.1 %collective-permute-done = f32[64,6,1024]{2,0,1:T(8,128)} collective-permute-done((f32[64,6,1024]{2,0,1:T(8,128)S(1)}, f32[64,6,1024]{2,0,1:T(8,128)}, u32[]{:S(2)}, u32[]{:S(2)}) %collective-permute-start) | collective-permute-done | bytes 1572896 | tf_op jit(solution)/shard_map/ppermute | solution.py:41
  50.7 2.7 constant_dynamic-update-slice_fusion.2
  53.5 6.6 %constant_dynamic-update-slice_fusion.1 = f32[64,28,1024]{2,0,1:T(8,128)} fusion(f32[64,28,1024]{2,0,1:T(8,128)} %constant_dynamic-update-slice_fusion.2, f32[64,16,1024]{2,1,0:T(8,128)} %param.10), kind=kLoop, calls=%fused_computation.132 | loop fusion | bytes 8388608
  60.1 23.4 %collective-permute-done.1 = f32[64,6,1024]{2,0,1:T(8,128)} collective-permute-done((f32[64,6,1024]{2,0,1:T(8,128)S(1)}, f32[64,6,1024]{2,0,1:T(8,128)}, u32[]{:S(2)}, u32[]{:S(2)}) %collective-permute-start.1) | collective-permute-done | bytes 1572896 | tf_op jit(solution)/shard_map/ppermute | solution.py:42
  83.5 2.8 constant_dynamic-update-slice_fusion
  86.4 11.1 %copy.39 = f32[64,28,1024]{0,2,1:T(8,128)} copy(f32[64,28,1024]{2,0,1:T(8,128)} %constant_dynamic-update-slice_fusion) | data formatting | bytes 14680064 | tf_op jit(solution)/shard_map/concatenate | solution.py:43
  97.5 33.1 %gather_fusion = f32[8192,64]{1,0:T(8,128)} fusion(f32[64,28672]{0,1:T(8,128)} %bitcast.72, s32[8192]{0:T(1024)S(1)} %broadcast_clamp_fusion), kind=kCustom, calls=%fused_computation | custom fusion | bytes 4227072 | tf_op jit(solution)/shard_map/gather | solution.py:98
  130.5 2.8 copy.40
  133.4 1.8 fusion.62
  135.2 1.9 convolution_bitcast_fusion
  137.1 0.2 copy.54
  137.3 2.7 copy.43
  140.0 50.9 %scatter_custom_fusion = f32[64,28672]{0,1:T(8,128)} fusion(s32[8192]{0:T(1024)S(1)} %bitcast.81, f32[8192,64]{1,0:T(8,128)} %copy.43, f32[]{:T(128)} %constant.181.clone.1), kind=kCustom, calls=%fused_computation.28 | custom fusion | flops 524288 | bytes 7340544 | tf_op jit(solution)/shard_map/scatter-add | solution.py:57
  190.9 7.1 %fusion.94 = (f32[64,6,1024]{0,2,1:T(8,128)}, f32[64,6,1024]{0,2,1:T(8,128)}, f32[64,6,1024]{0,2,1:T(8,128)S(1)}) fusion(f32[64,28,1024]{0,2,1:T(8,128)} %bitcast.70), kind=kLoop, calls=%fused_computation.166 | loop fusion | bytes 9437184 | tf_op jit(solution)/shard_map/slice | solution.py:62
  198.0 3.3 copy.52
  201.3 0.6 collective-permute-start.2
  201.8 3.2 copy.53
  205.1 10.5 %collective-permute-start.3 = (f32[64,6,1024]{2,0,1:T(8,128)}, f32[64,6,1024]{2,0,1:T(8,128)}, u32[]{:S(2)}, u32[]{:S(2)}) collective-permute-start(f32[64,6,1024]{2,0,1:T(8,128)} %copy.53), channel_id=1, source_target_pairs={{8,0},{16,8},{24,16},{0,24},{9,1},{17,9},{25,17},{1,25},{10,2},{18... | collective-permute-start | bytes 4718600 | tf_op jit(solution)/shard_map/ppermute | solution.py:31
  215.6 7.5 %slice.277 = f32[64,16,1024]{0,2,1:T(8,128)} slice(f32[64,28,1024]{0,2,1:T(8,128)} %bitcast.71), slice={[0:64], [6:22], [0:1024]} | slice | bytes 8388608 | tf_op jit(solution)/shard_map/slice | solution.py:63
  223.1 2.0 copy.51
  225.1 6.9 %copy.50 = f32[64,16,1024]{2,0,1:T(8,128)} copy(f32[64,16,1024]{0,2,1:T(8,128)} %slice.277) | data formatting | bytes 8388608
  232.0 15.9 %collective-permute-done.2 = f32[64,6,1024]{2,0,1:T(8,128)} collective-permute-done((f32[64,6,1024]{2,0,1:T(8,128)}, f32[64,6,1024]{2,0,1:T(8,128)}, u32[]{:S(2)}, u32[]{:S(2)}) %collective-permute-start.2) | collective-permute-done | bytes 1572896 | tf_op jit(solution)/shard_map/ppermute | solution.py:31
  247.9 2.8 add_dynamic-update-slice_fusion
  250.8 22.7 %collective-permute-done.3 = f32[64,6,1024]{2,0,1:T(8,128)} collective-permute-done((f32[64,6,1024]{2,0,1:T(8,128)}, f32[64,6,1024]{2,0,1:T(8,128)}, u32[]{:S(2)}, u32[]{:S(2)}) %collective-permute-start.3) | collective-permute-done | bytes 1572896 | tf_op jit(solution)/shard_map/ppermute | solution.py:31
  273.4 3.4 fusion.58
  276.8 0.0 reduce-scatter.2.cloned.1.call-update
  276.9 0.0 all-gather.3.cloned.1.call-start
  277.0 1.7 constant_dynamic-slice_fusion.1
  278.7 8.5 %reduce-scatter.2.cloned.1.call-done = f32[64,8,1024]{2,0,1:T(8,128)} async-done(((f32[64,16,1024]{2,0,1:T(8,128)}), f32[64,8,1024]{2,0,1:T(8,128)}) %reduce-scatter.2.cloned.1.call-update) | async-done | bytes 2097168 | tf_op jit(solution)/shard_map/reduce_scatter | solution.py:106
  287.3 15.7 %fusion.57 = f32[8,8,8,1024]{3,2,1,0:T(8,128)S(1)} fusion(f32[64,8,1024]{2,0,1:T(8,128)S(1)} %constant_dynamic-slice_fusion.1, f32[64,8,1024]{2,0,1:T(8,128)} %reduce-scatter.2.cloned.1.call-done, f32[64,28,1024]{2,0,1:T(8,128)} %constant_dynamic-update-slice_fusion, s32[]{:T(128)S(6)} %select_n.94, s32[]{:T(128)S(6)} %add.299, s32[]{:T(128)S(6)} %add.298, ...), kind=kLoop, calls=%fused_computation.91 | loop fusion | flops 31981568 | bytes 31502384
  303.0 1.6 copy.55
  304.5 0.0 all-gather.3.cloned.1.call-update
  304.6 88.9 %all-gather.3.cloned.1.call-done = f32[256,8192]{1,0:T(8,128)} async-done(((f32[64,8192]{1,0:T(8,128)}), f32[256,8192]{1,0:T(8,128)}) %all-gather.3.cloned.1.call-update) | async-done | bytes 8388624 | tf_op jit(solution)/shard_map/all_gather | solution.py:112
  393.5 10.1 %fusion.96 = f32[64,256]{1,0:T(8,128)S(1)} fusion(f32[64,8192]{1,0:T(8,128)S(1)} %bitcast.74, f32[256,8192]{1,0:T(8,128)} %all-gather.3.cloned.1.call-done), kind=kOutput, calls=%fused_computation.168 | convolution fusion | flops 1610612736 | bytes 10551296 | tf_op jit(solution)/shard_map/dot_general | solution.py:48
  403.6 14.7 %all-gather = f32[512,256]{1,0:T(8,128)S(1)} all-gather(f32[64,256]{1,0:T(8,128)S(1)} %fusion.96), channel_id=2, replica_groups=mesh['grid'=4,'band'=4,'atom'=2] {'grid','atom'}, dimensions={0}, use_global_device_ids=true | all-gather | bytes 589824 | tf_op jit(solution)/shard_map/all_gather | solution.py:24
  418.4 9.1 %all_gather.16 = f32[256,256]{1,0:T(8,128)S(1)} all-gather(f32[64,256]{1,0:T(8,128)S(1)} %broadcast_multiply_fusion), channel_id=1, replica_groups=mesh['grid'=4,'band'=4,'atom'=2] {'band'}, dimensions={0}, use_global_device_ids=true | all-gather | bytes 327680 | tf_op jit(solution)/shard_map/all_gather | solution.py:114
  427.5 0.1 copy.49
  427.7 11.7 %cholesky.50 = f32[128,128]{1,0:T(8,128)S(1)} custom-call(f32[128,128]{1,0:T(8,128)S(1)} %cholesky.118), custom_call_target="Cholesky" | custom-call | tf_op jit(solution)/shard_map/jit(cholesky)/cholesky | solution.py:115
  439.5 9.8 %custom-call.14 = f32[1,128,128]{1,2,0:T(8,128)S(1)} custom-call(f32[1,128,128]{2,1,0:T(8,128)S(1)} %get-tuple-element.55), custom_call_target="InvertDiagBlocksLowerTriangular" | custom-call | tf_op jit(solution)/shard_map/jit(cholesky)/cholesky | solution.py:115
  449.3 0.2 constant_dynamic-update-slice_fusion.3
  449.5 0.3 convolution_subtract_fusion.1
  449.8 11.7 %cholesky.105 = f32[128,128]{1,0:T(8,128)S(1)} custom-call(f32[128,128]{1,0:T(8,128)S(1)} %convolution_subtract_fusion.1), custom_call_target="Cholesky" | custom-call | tf_op jit(solution)/shard_map/jit(cholesky)/cholesky | solution.py:115
  461.5 0.7 compare_reduce_fusion
  462.2 0.6 compare_reduce_fusion.1
  464.2 0.1 triangular_solve.63
  464.2 4.1 while.3
  464.4 0.6 fusion.106
  465.0 1.4 bitcast_dynamic-update-slice_fusion.2
  466.4 0.6 fusion.106
  467.0 1.4 bitcast_dynamic-update-slice_fusion.2
  468.4 19.7 %custom-call.15 = f32[2,128,128]{1,2,0:T(8,128)S(1)} custom-call(f32[2,128,128]{2,1,0:T(8,128)S(1)} %get-tuple-element.36), custom_call_target="InvertDiagBlocksLowerTriangular" | custom-call | tf_op jit(solution)/shard_map/triangular_solve | solution.py:116
  488.1 0.3 fusion.66
  488.3 0.3 convolution_subtract_fusion
  488.6 0.3 fusion.74
  488.9 7.5 %fusion.71 = f32[64,8192]{1,0:T(8,128)S(1)} fusion(f32[256,8192]{1,0:T(8,128)} %all-gather.3.cloned.1.call-done, s32[]{:T(128)S(6)} %select_n.112, f32[128,256]{1,0:T(8,128)S(1)} %fusion.66, f32[128,256]{1,0:T(8,128)S(1)} %fusion.74), kind=kOutput, calls=%fused_computation.114 | convolution fusion | flops 1610629120 | bytes 10747908 | tf_op jit(solution)/shard_map/dot_general | solution.py:122
  496.4 2.5 copy.58
  (40 shorter events, 0.4 us)
Async XLA Ops:
  6.5 126.8 %copy-start = (f32[32,4,512]{2,1,0:T(4,128)S(1)}, f32[32,4,512]{2,1,0:T(4,128)}, u32[]{:S(2)}) copy-start(f32[32,4,512]{2,1,0:T(4,128)} %param.12) | copy-start | bytes 786436
  6.5 280.7 %reduce-scatter.2.cloned.1.call-start = ((), (), s32[]{:S(2)}) async-start(), calls=%async_computation.1 | async-start | bytes 6291456 | tf_op jit(solution)/shard_map/reduce_scatter | solution.py:106
  10.2 6.4 %copy-start.5 = (s32[32,512]{1,0:T(8,128)S(1)}, s32[32,512]{1,0:T(8,128)}, u32[]{:S(2)}) copy-start(s32[32,512]{1,0:T(8,128)} %param.14) | copy-start | bytes 196612
  10.2 7.2 %copy-start.6 = (f32[32,4]{0,1:T(4,128)S(1)}, f32[32,4]{0,1:T(4,128)}, u32[]{:S(2)}) copy-start(f32[32,4]{0,1:T(4,128)} %param.13) | copy-start | bytes 1540
  10.2 40.5 %collective-permute-start = (f32[64,6,1024]{2,0,1:T(8,128)S(1)}, f32[64,6,1024]{2,0,1:T(8,128)}, u32[]{:S(2)}, u32[]{:S(2)}) collective-permute-start(f32[64,6,1024]{2,0,1:T(8,128)S(1)} %copy.60), channel_id=1, source_target_pairs={{0,8},{8,16},{16,24},{24,0},{1,9},{9,17},{17,25},{25,1},{2,10},{10... | collective-permute-start | bytes 4718600 | tf_op jit(solution)/shard_map/ppermute | solution.py:41
  14.2 69.3 %collective-permute-start.1 = (f32[64,6,1024]{2,0,1:T(8,128)S(1)}, f32[64,6,1024]{2,0,1:T(8,128)}, u32[]{:S(2)}, u32[]{:S(2)}) collective-permute-start(f32[64,6,1024]{2,0,1:T(8,128)S(1)} %copy.61), channel_id=1, source_target_pairs={{8,0},{16,8},{24,16},{0,24},{9,1},{17,9},{25,17},{1,25},{10,2},{18... | collective-permute-start | bytes 4718600 | tf_op jit(solution)/shard_map/ppermute | solution.py:42
  201.3 46.7 %collective-permute-start.2 = (f32[64,6,1024]{2,0,1:T(8,128)}, f32[64,6,1024]{2,0,1:T(8,128)}, u32[]{:S(2)}, u32[]{:S(2)}) collective-permute-start(f32[64,6,1024]{2,0,1:T(8,128)} %copy.52), channel_id=1, source_target_pairs={{24,0},{0,8},{8,16},{16,24},{25,1},{1,9},{9,17},{17,25},{26,2},{2,... | collective-permute-start | bytes 4718600 | tf_op jit(solution)/shard_map/ppermute | solution.py:31
  205.1 68.4 %collective-permute-start.3 = (f32[64,6,1024]{2,0,1:T(8,128)}, f32[64,6,1024]{2,0,1:T(8,128)}, u32[]{:S(2)}, u32[]{:S(2)}) collective-permute-start(f32[64,6,1024]{2,0,1:T(8,128)} %copy.53), channel_id=1, source_target_pairs={{8,0},{16,8},{24,16},{0,24},{9,1},{17,9},{25,17},{1,25},{10,2},{18... | collective-permute-start | bytes 4718600 | tf_op jit(solution)/shard_map/ppermute | solution.py:31
  225.1 22.8 %copy-start.3 = (f32[64,6,1024]{2,0,1:T(8,128)S(1)}, f32[64,6,1024]{2,0,1:T(8,128)}, u32[]{:S(2)}) copy-start(f32[64,6,1024]{2,0,1:T(8,128)} %copy.51) | copy-start | bytes 4718596
  276.9 116.6 %all-gather.3.cloned.1.call-start = ((), (), s32[]{:S(2)}) async-start(), calls=%async_computation.2 | async-start | bytes 10485760 | tf_op jit(solution)/shard_map/all_gather | solution.py:112
  277.0 10.3 %copy-start.4 = (f32[8,1024]{1,0:T(8,128)S(1)}, f32[8,1024]{1,0:T(8,128)}, u32[]{:S(2)}) copy-start(f32[8,1024]{1,0:T(8,128)} %param.11) | copy-start | bytes 98308
  304.5 89.0 %copy-start.2 = (f32[8,8,8,1024]{3,2,0,1:T(8,128)S(1)}, f32[8,8,8,1024]{3,2,0,1:T(8,128)}, u32[]{:S(2)}) copy-start(f32[8,8,8,1024]{3,2,0,1:T(8,128)} %copy.55) | copy-start | bytes 6291460
  496.4 2.5 copy-start.1
Sparse Core Ops, SparseCore 0:
  277.0 10.2 reduce-scatter.1
  304.7 88.7 all-gather.2
